TPU v7x, 32 devices: a whole 2x2x4 slice. The times are simulated.
32 devices in a mesh: blk: 8 (over z, x), col: 4 (over y, core).
Axes of the slice: x: 2, y: 2, z: 4, core: 2. Of those that a mesh axis runs over, the one named last changes fastest.
Arguments:
- points: bfloat16 [4096, 128], P(('blk', 'col')), may hold values from -4.5 to 4.5
- targets: float32 [4096, 32], P(('blk', 'col')), may hold values from -6 to 6
- pivots: int32 [2, 256], replicated, may hold values from 0 to 4095, as said below
Outputs:
- factor: bfloat16 [4096, 512], P(('blk', 'col'))
- solution: float32 [4096, 32], P(('blk', 'col'))
- residual: float32 [4096, 32], P(('blk', 'col'))
Inputs may be any that keep to these rules, and one draw needn't show every extreme that they name: `pivots`: the 512 indices are distinct; 0 and 4095 are among them.
All inputs are finite; a program needn't handle non-finite values.
Results may differ from a plain program's by a relative error of at most 0.012.
Values may be sent and summed in bfloat16 or wider, within the bound.
A program may use at most 64 MiB of HBM per device.

v0:
```python
import jax
import jax.numpy as jnp
from jax import lax
from jax.sharding import PartitionSpec as P

FEATURES = 128
ITERS = 3
noise_level = 0.5
jitter_level = 0.05
highest = lax.Precision.HIGHEST


def squared_norms(point_rows):
    wide_rows = point_rows.astype(jnp.float32)
    return jnp.sum(wide_rows * wide_rows, axis=1)


def kernel_block(left_rows, left_norms, right_rows, right_norms):
    inner = lax.dot_general(
        left_rows, right_rows, (((1,), (1,)), ((), ())), preferred_element_type=jnp.float32
    )
    distance = left_norms[:, None] + right_norms[None, :] - 2.0 * inner
    return jnp.exp(-2.0 * distance / FEATURES)


def lower_solve(lower_factor, right_rows):
    return jax.scipy.linalg.solve_triangular(lower_factor, right_rows.T, lower=True).T


def build_factor(point_rows, first_pick, second_pick):
    row_norms = squared_norms(point_rows)
    first_norms = squared_norms(first_pick)
    second_norms = squared_norms(second_pick)
    identity_piv = jnp.eye(first_pick.shape[0], dtype=jnp.float32)
    first_chol = jnp.linalg.cholesky(
        kernel_block(first_pick, first_norms, first_pick, first_norms) + jitter_level * identity_piv
    )
    first_coef = lower_solve(
        first_chol, kernel_block(point_rows, row_norms, first_pick, first_norms)
    )
    shared_coef = lower_solve(
        first_chol, kernel_block(second_pick, second_norms, first_pick, first_norms)
    )
    schur_block = (
        kernel_block(second_pick, second_norms, second_pick, second_norms)
        + jitter_level * identity_piv
        - jnp.dot(shared_coef, shared_coef.T, precision=highest)
    )
    second_chol = jnp.linalg.cholesky(schur_block)
    second_cross = kernel_block(point_rows, row_norms, second_pick, second_norms) - jnp.dot(
        first_coef, shared_coef.T, precision=highest
    )
    second_coef = lower_solve(second_chol, second_cross)
    return jnp.concatenate([first_coef, second_coef], axis=1)


def per_device(points, targets, pivots):
    row_count = points.shape[0]
    piv_count = pivots.shape[1]
    shard_index = lax.axis_index("blk") * lax.axis_size("col") + lax.axis_index("col")
    first_row = shard_index * row_count
    flat_pivots = pivots.reshape(-1)
    owned = (
        flat_pivots[:, None] == first_row + jnp.arange(row_count, dtype=jnp.int32)[None, :]
    ).astype(jnp.float32)
    local_pick = jnp.dot(owned, points.astype(jnp.float32), precision=highest)
    picked = lax.psum(local_pick, ("blk", "col")).astype(jnp.bfloat16)
    wide_factor = build_factor(points, picked[:piv_count], picked[piv_count:])
    factor = wide_factor.astype(jnp.bfloat16)
    local_gram = lax.dot_general(
        wide_factor, wide_factor, (((0,), (0,)), ((), ())), precision=highest
    )
    gram = lax.psum(local_gram, ("blk", "col"))
    gram = gram + noise_level * jnp.eye(2 * piv_count, dtype=jnp.float32)
    gram_chol = jnp.linalg.cholesky(gram)

    def precondition(residual_now):
        local_proj = lax.dot_general(
            wide_factor, residual_now, (((0,), (0,)), ((), ())), precision=highest
        )
        square_sum, projection = lax.psum(
            (jnp.sum(residual_now * residual_now, axis=0), local_proj), ("blk", "col")
        )
        coefficients = jax.scipy.linalg.cho_solve((gram_chol, True), projection)
        scaled = (
            residual_now - jnp.dot(wide_factor, coefficients, precision=highest)
        ) / noise_level
        return (scaled, (square_sum - jnp.sum(projection * coefficients, axis=0)) / noise_level)

    own_block = lax.all_gather(points, "col", axis=0, tiled=True)
    own_norms = squared_norms(own_block)

    def tile_add(total, key_rows, key_norms, direction_rows):
        weights = kernel_block(own_block, own_norms, key_rows, key_norms)
        return total + jnp.dot(weights, direction_rows, precision=highest)

    solution = jnp.zeros_like(targets)
    residual = targets
    direction_now, inner_now = precondition(residual)
    for step_index in range(ITERS):
        empty = jnp.zeros((own_block.shape[0], direction_now.shape[1]), jnp.float32)
        add_key_rows = lax.all_gather(points.astype(jnp.float32), "blk", axis=0, tiled=True).astype(
            jnp.bfloat16
        )
        fold_direction_rows = lax.all_gather(direction_now, "blk", axis=0, tiled=True)
        piece_rows = add_key_rows.shape[0]
        splits = piece_rows // row_count

        def scan_step(carry, operands):
            return (tile_add(carry, operands[0], operands[1], operands[2]), None)

        stacked = (
            add_key_rows.reshape(splits, row_count, add_key_rows.shape[1]),
            squared_norms(add_key_rows).reshape(splits, row_count),
            fold_direction_rows.reshape(splits, row_count, fold_direction_rows.shape[1]),
        )
        result, unused = lax.scan(scan_step, empty, stacked)
        image = (
            lax.psum_scatter(result, "col", scatter_dimension=0, tiled=True)
            + noise_level * direction_now
        )
        curvature = lax.psum(jnp.sum(direction_now * image, axis=0), ("blk", "col"))
        step_size = inner_now / curvature
        solution = solution + step_size * direction_now
        residual = residual - step_size * image
        if step_index + 1 < ITERS:
            scaled, inner_next = precondition(residual)
            direction_now = scaled + inner_next / inner_now * direction_now
            inner_now = inner_next
    return (factor, solution, residual)


def solution(mesh):
    return jax.shard_map(
        per_device,
        mesh=mesh,
        in_specs=(P(("blk", "col"), None), P(("blk", "col"), None), P()),
        out_specs=(P(("blk", "col"), None), P(("blk", "col"), None), P(("blk", "col"), None)),
        check_vma=False,
    )
```

profile of v0, /device:TPU:0, one launch (start us, length us, event | category | flops | bytes accessed | tf_op | source)
XLA Modules:
  0.0 1023.6 jit_solution(6104249524737897158)
XLA Ops:
  8.9 44.6 %all-reduce.14 = bf16[512,128]{1,0:T(8,128)(2,1)S(1)} all-reduce(f32[512,128]{1,0:T(8,128)S(1)} %fusion.59), channel_id=1, replica_groups=mesh['blk'=8,'col'=4] {'blk','col'}, use_global_device_ids=true, to_apply=%region_0.0 | all-reduce | flops 65536 | bytes 393216 | tf_op jit(solution)/shard_map/psum | solution.py:67
  54.1 11.7 %cholesky.354 = f32[128,128]{1,0:T(8,128)S(1)} custom-call(f32[128,128]{1,0:T(8,128)S(1)} %cholesky.404), custom_call_target="Cholesky" | custom-call | tf_op jit(solution)/shard_map/jit(cholesky)/cholesky | solution.py:35
  76.4 11.7 %cholesky.364 = f32[128,128]{1,0:T(8,128)S(1)} custom-call(f32[128,128]{1,0:T(8,128)S(1)} %convolution_subtract_fusion.8), custom_call_target="Cholesky" | custom-call | tf_op jit(solution)/shard_map/jit(cholesky)/cholesky | solution.py:35
  96.3 19.7 %custom-call.55 = f32[2,128,128]{1,2,0:T(8,128)S(1)} custom-call(f32[2,128,128]{2,1,0:T(8,128)S(1)} %get-tuple-element.391), custom_call_target="InvertDiagBlocksLowerTriangular" | custom-call | tf_op jit(solution)/shard_map/jit(_solve_triangular)/triangular_solve | solution.py:27
  118.7 11.7 %cholesky.381 = f32[128,128]{1,0:T(8,128)S(1)} custom-call(f32[128,128]{1,0:T(8,128)S(1)} %cholesky.407), custom_call_target="Cholesky" | custom-call | tf_op jit(solution)/shard_map/jit(cholesky)/cholesky | solution.py:49
  140.8 11.7 %cholesky.391 = f32[128,128]{1,0:T(8,128)S(1)} custom-call(f32[128,128]{1,0:T(8,128)S(1)} %convolution_subtract_fusion.6), custom_call_target="Cholesky" | custom-call | tf_op jit(solution)/shard_map/jit(cholesky)/cholesky | solution.py:49
  159.6 19.7 %custom-call.57 = f32[2,128,128]{1,2,0:T(8,128)S(1)} custom-call(f32[2,128,128]{2,1,0:T(8,128)S(1)} %get-tuple-element.392), custom_call_target="InvertDiagBlocksLowerTriangular" | custom-call | tf_op jit(solution)/shard_map/jit(_solve_triangular)/triangular_solve | solution.py:27
  189.2 31.2 %all_gather.18 = bf16[1024,128]{1,0:T(8,128)(2,1)S(1)} all-gather(bf16[128,128]{1,0:T(8,128)(2,1)S(1)} %copy-done.6), channel_id=1, replica_groups=mesh['blk'=8,'col'=4] {'blk'}, dimensions={0}, use_global_device_ids=true | all-gather | bytes 294912 | tf_op jit(solution)/shard_map/all_gather | solution.py:102
  221.3 93.0 %all-reduce.13.cloned.1.call-done = (f32[512,512]{1,0:T(8,128)}, f32[512,32]{0,1:T(8,128)}) async-done(((f32[512,512]{1,0:T(8,128)}, f32[512,32]{0,1:T(8,128)}), (f32[512,512]{1,0:T(8,128)}, f32[512,32]{0,1:T(8,128)})) %all-reduce.13.cloned.1.call-update) | async-done | bytes 1114128 | tf_op jit(solution)/shard_map/psum | solution.py:73
  317.1 11.7 %cholesky.166 = f32[128,128]{1,0:T(8,128)S(1)} custom-call(f32[128,128]{1,0:T(8,128)S(1)} %cholesky.410), custom_call_target="Cholesky" | custom-call | tf_op jit(solution)/shard_map/jit(cholesky)/cholesky | solution.py:75
  339.5 11.7 %cholesky.189 = f32[128,128]{1,0:T(8,128)S(1)} custom-call(f32[128,128]{1,0:T(8,128)S(1)} %cholesky.414), custom_call_target="Cholesky" | custom-call | tf_op jit(solution)/shard_map/jit(cholesky)/cholesky | solution.py:75
  352.5 9.9 custom-call.43
  363.1 11.7 %cholesky.292 = f32[128,128]{1,0:T(8,128)S(1)} custom-call(f32[128,128]{1,0:T(8,128)S(1)} %cholesky.419), custom_call_target="Cholesky" | custom-call | tf_op jit(solution)/shard_map/jit(cholesky)/cholesky | solution.py:75
  386.0 11.9 %cholesky.305 = f32[128,128]{1,0:T(8,128)S(1)} custom-call(f32[128,128]{1,0:T(8,128)S(1)} %convolution_subtract_fusion.9), custom_call_target="Cholesky" | custom-call | tf_op jit(solution)/shard_map/jit(cholesky)/cholesky | solution.py:75
  401.3 10.4 %while.55 = (s32[]{:T(128)}, f32[512,512]{1,0:T(8,128)S(1)}, s32[4,2]{0,1:T(2,128)S(1)}, f32[4,128,128]{2,1,0:T(8,128)}, s32[]{:T(128)}) while((s32[]{:T(128)}, f32[512,512]{1,0:T(8,128)S(1)}, s32[4,2]{0,1:T(2,128)S(1)}, f32[4,128,128]{2,1,0:T(8,128)}, s32[]{:T(128)}) %tuple.173), condition=%wide.while_cond.1, body=%wide.while_body.1.sunk | while | flops 2 | bytes 132705 | solution.py:84
  411.7 40.1 %custom-call.59 = f32[4,128,128]{1,2,0:T(8,128)S(1)} custom-call(f32[4,128,128]{2,1,0:T(8,128)} %get-tuple-element.393), custom_call_target="InvertDiagBlocksLowerTriangular" | custom-call | tf_op jit(solution)/shard_map/jit(_cho_solve)/triangular_solve | solution.py:84
  455.8 30.6 %all_gather.19 = f32[1024,32]{0,1:T(8,128)S(1)} all-gather(f32[128,32]{0,1:T(8,128)S(1)} %get-tuple-element.538), channel_id=1, replica_groups=mesh['blk'=8,'col'=4] {'blk'}, dimensions={0}, use_global_device_ids=true | all-gather | bytes 147456 | tf_op jit(solution)/shard_map/all_gather | solution.py:105
  487.2 11.4 %while.50 = (s32[]{:T(128)}, f32[512,32]{0,1:T(8,128)S(1)}, f32[512]{0:T(512)S(1)}, f32[8,128]{1,0:T(8,128)S(1)}, bf16[8,128,128]{2,1,0:T(8,128)(2,1)}, /*index=...) while((s32[]{:T(128)}, f32[512,32]{0,1:T(8,128)S(1)}, ...), condition=%wide.region_24.29_spmd.clone, body=%wide.region_23.28_spmd.clone.sunk | while | flops 42237952 | bytes 888943 | solution.py:117
  499.5 19.3 %reduce-scatter.4.cloned.1.call-done = f32[128,32]{0,1:T(8,128)} async-done(((f32[512,32]{0,1:T(8,128)}), f32[128,32]{0,1:T(8,128)}) %reduce-scatter.4.cloned.1.call-update) | async-done | bytes 16400 | tf_op jit(solution)/shard_map/reduce_scatter | solution.py:119
  519.6 39.3 %all-reduce.2 = (f32[32]{0:T(128)S(1)}, f32[32]{0:T(128)S(1)}) all-reduce(f32[32]{0:T(128)S(1)} %get-tuple-element.506, f32[32]{0:T(128)S(1)} %multiply_reduce_fusion.13), channel_id=1, replica_groups=mesh['blk'=8,'col'=4] {'blk','col'}, use_global_device_ids=true, to_apply=%region_27.32 | all-reduce | flops 64 | bytes 512 | tf_op jit(solution)/shard_map/psum | solution.py:122
  560.2 41.0 %psum.82 = f32[32]{0:T(128)S(1)} all-reduce(f32[32]{0:T(128)S(1)} %get-tuple-element.504), channel_id=1, replica_groups=mesh['blk'=8,'col'=4] {'blk','col'}, use_global_device_ids=true, to_apply=%region_29.34 | all-reduce | flops 32 | bytes 256 | tf_op jit(solution)/shard_map/psum | solution.py:81
  601.2 79.3 %all-reduce.9.cloned.1.call-done = f32[512,32]{0,1:T(8,128)} async-done(((f32[512,32]{0,1:T(8,128)}), f32[512,32]{0,1:T(8,128)}) %all-reduce.9.cloned.1.call-update) | async-done | bytes 65552 | tf_op jit(solution)/shard_map/psum | solution.py:81
  684.9 30.5 %all_gather.20 = f32[1024,32]{0,1:T(8,128)S(1)} all-gather(f32[128,32]{0,1:T(8,128)S(1)} %fusion.53), channel_id=1, replica_groups=mesh['blk'=8,'col'=4] {'blk'}, dimensions={0}, use_global_device_ids=true | all-gather | bytes 147456 | tf_op jit(solution)/shard_map/all_gather | solution.py:105
  715.6 11.4 %while.51 = (s32[]{:T(128)}, f32[512,32]{0,1:T(8,128)S(1)}, f32[512]{0:T(512)S(1)}, f32[8,128]{1,0:T(8,128)S(1)}, bf16[8,128,128]{2,1,0:T(8,128)(2,1)}, /*index=...) while((s32[]{:T(128)}, f32[512,32]{0,1:T(8,128)S(1)}, ...), condition=%wide.region_33.38_spmd.clone, body=%wide.region_32.37_spmd.clone.sunk | while | flops 42237952 | bytes 888943 | solution.py:117
  727.7 19.1 %reduce-scatter.6.cloned.1.call-done = f32[128,32]{0,1:T(8,128)} async-done(((f32[512,32]{0,1:T(8,128)}), f32[128,32]{0,1:T(8,128)}) %reduce-scatter.6.cloned.1.call-update) | async-done | bytes 16400 | tf_op jit(solution)/shard_map/reduce_scatter | solution.py:119
  747.7 39.3 %psum.84 = f32[32]{0:T(128)S(1)} all-reduce(f32[32]{0:T(128)S(1)} %multiply_reduce_fusion.10), channel_id=1, replica_groups=mesh['blk'=8,'col'=4] {'blk','col'}, use_global_device_ids=true, to_apply=%region_36.41 | all-reduce | flops 32 | bytes 256 | tf_op jit(solution)/shard_map/psum | solution.py:122
  788.3 41.2 %psum.85 = f32[32]{0:T(128)S(1)} all-reduce(f32[32]{0:T(128)S(1)} %get-tuple-element.502), channel_id=1, replica_groups=mesh['blk'=8,'col'=4] {'blk','col'}, use_global_device_ids=true, to_apply=%region_38.43 | all-reduce | flops 32 | bytes 256 | tf_op jit(solution)/shard_map/psum | solution.py:81
  829.5 79.0 %all-reduce.11.cloned.1.call-done = f32[512,32]{0,1:T(8,128)} async-done(((f32[512,32]{0,1:T(8,128)}), f32[512,32]{0,1:T(8,128)}) %all-reduce.11.cloned.1.call-update) | async-done | bytes 65552 | tf_op jit(solution)/shard_map/psum | solution.py:81
  912.9 30.5 %all_gather.21 = f32[1024,32]{0,1:T(8,128)S(1)} all-gather(f32[128,32]{0,1:T(8,128)S(1)} %fusion.54), channel_id=1, replica_groups=mesh['blk'=8,'col'=4] {'blk'}, dimensions={0}, use_global_device_ids=true | all-gather | bytes 147456 | tf_op jit(solution)/shard_map/all_gather | solution.py:105
  943.6 11.4 %while.52 = (s32[]{:T(128)}, f32[512,32]{0,1:T(8,128)S(1)}, f32[512]{0:T(512)S(1)}, f32[8,128]{1,0:T(8,128)S(1)}, bf16[8,128,128]{2,1,0:T(8,128)(2,1)}, /*index=...) while((s32[]{:T(128)}, f32[512,32]{0,1:T(8,128)S(1)}, ...), condition=%wide.region_42.47_spmd.clone, body=%wide.region_41.46_spmd.clone.sunk | while | flops 42237952 | bytes 888943 | solution.py:117
  955.7 19.1 %reduce-scatter.8.cloned.1.call-done = f32[128,32]{0,1:T(8,128)} async-done(((f32[512,32]{0,1:T(8,128)}), f32[128,32]{0,1:T(8,128)}) %reduce-scatter.8.cloned.1.call-update) | async-done | bytes 16400 | tf_op jit(solution)/shard_map/reduce_scatter | solution.py:119
  976.4 39.2 %psum.87 = f32[32]{0:T(128)S(1)} all-reduce(f32[32]{0:T(128)S(1)} %multiply_reduce_fusion.8), channel_id=1, replica_groups=mesh['blk'=8,'col'=4] {'blk','col'}, use_global_device_ids=true, to_apply=%region_45.50 | all-reduce | flops 32 | bytes 256 | tf_op jit(solution)/shard_map/psum | solution.py:122
  (299 shorter events, 150.5 us)
Async XLA Ops:
  7.2 307.2 %all-reduce.13.cloned.1.call-start = ((), (), s32[]{:S(2)}) async-start(), calls=%async_computation.8 | async-start | bytes 2228224 | tf_op jit(solution)/shard_map/psum | solution.py:73
  7.2 0.7 copy-start.14
  88.1 0.8 copy-start.6
  180.7 2.0 copy-start.10
  183.7 335.1 %reduce-scatter.4.cloned.1.call-start = ((), (), s32[]{:S(2)}) async-start(), calls=%async_computation.3 | async-start | bytes 81920 | tf_op jit(solution)/shard_map/reduce_scatter | solution.py:119
  220.4 0.7 copy-start.1
  315.7 1.2 copy-start
  401.3 50.6 %copy-start.7 = (f32[512,32]{0,1:T(8,128)S(1)}, f32[512,32]{0,1:T(8,128)}, u32[]{:S(2)}) copy-start(f32[512,32]{0,1:T(8,128)} %get-tuple-element.499) | copy-start | bytes 196612
  454.8 0.7 copy-start.11
  486.4 0.8 copy-start.2
  498.6 0.6 copy-start.3
  499.2 181.2 %all-reduce.9.cloned.1.call-start = ((), (), s32[]{:S(2)}) async-start(), calls=%async_computation.4 | async-start | bytes 131072 | tf_op jit(solution)/shard_map/psum | solution.py:81
  560.2 186.6 %reduce-scatter.6.cloned.1.call-start = ((), (), s32[]{:S(2)}) async-start(), calls=%async_computation.5 | async-start | bytes 81920 | tf_op jit(solution)/shard_map/reduce_scatter | solution.py:119
  680.5 1.0 copy-start.9
  727.0 0.6 copy-start.5
  727.7 180.8 %all-reduce.11.cloned.1.call-start = ((), (), s32[]{:S(2)}) async-start(), calls=%async_computation.6 | async-start | bytes 131072 | tf_op jit(solution)/shard_map/psum | solution.py:81
  746.8 40.2 %copy-start.13 = (f32[128,32]{0,1:T(8,128)S(1)}, f32[128,32]{0,1:T(8,128)}, u32[]{:S(2)}) copy-start(f32[128,32]{0,1:T(8,128)} %reduce-scatter.6.cloned.1.call-done) | copy-start | bytes 49156
  788.2 186.6 %reduce-scatter.8.cloned.1.call-start = ((), (), s32[]{:S(2)}) async-start(), calls=%async_computation.7 | async-start | bytes 81920 | tf_op jit(solution)/shard_map/reduce_scatter | solution.py:119
  908.5 1.0 copy-start.8
  955.0 0.6 copy-start.4
  975.6 40.0 %copy-start.12 = (f32[128,32]{0,1:T(8,128)S(1)}, f32[128,32]{0,1:T(8,128)}, u32[]{:S(2)}) copy-start(f32[128,32]{0,1:T(8,128)} %reduce-scatter.8.cloned.1.call-done) | copy-start | bytes 49156
Sparse Core Ops, SparseCore 0:
  183.8 130.4 all-reduce.12
  499.3 19.4 reduce-scatter.3
  560.3 120.1 all-reduce.8
  727.8 18.9 reduce-scatter.5
  788.3 120.0 all-reduce.10
  955.8 18.9 reduce-scatter.7
where the time goes:
time: 1040 us; the launch traced here: 1020 us
  blocking collectives  373 us (36%)
  waiting for transfers between devices  309 us (30%)
  other arithmetic  234 us (22%)
  matrix products  58.3 us (6%)
  local copies, waits for them, and re-layouts  26.9 us (3%)
  between operations  20.8 us (2%)
    psum x2, waiting for transfers between devices, precondition(): lax.psum((jnp.sum(residual_now * residual_now, axis=0), local_proj), ('bl...  158 us
    psum x3, blocking collectives, per_device(): curvature = lax.psum(jnp.sum(direction_now * image, axis=0), ('blk', 'col'))  118 us
    psum x1, waiting for transfers between devices, per_device(): gram = lax.psum(local_gram, ('blk', 'col'))  93 us
    all_gather x3, blocking collectives, per_device(): lax.all_gather(direction_now, 'blk', axis=0, tiled=True)  91.6 us
    psum x2, blocking collectives, precondition(): lax.psum((jnp.sum(residual_now * residual_now, axis=0), local_proj), ('bl...  82.2 us
    another operation x15, other arithmetic, per_device(): gram_chol = jnp.linalg.cholesky(gram)  79.4 us
    reduce_scatter x3, waiting for transfers between devices, per_device(): lax.psum_scatter(result, 'col', scatter_dimension=0, tiled=True)  57.5 us
    psum x1, blocking collectives, per_device(): picked = lax.psum(local_pick, ('blk', 'col')).astype(jnp.bfloat16)  44.6 us
  transfers between devices with their start and end apart: 6, of which 6 were waited for; matrix products, arithmetic and copies ran while one was open for 0% of the time, Pallas kernels for 0%

commit v1 on v0

--- a/solution.py
+++ b/solution.py
@@ -79,7 +79,7 @@
             wide_factor, residual_now, (((0,), (0,)), ((), ())), precision=highest
         )
         square_sum, projection = lax.psum(
-            (jnp.sum(residual_now * residual_now, axis=0), local_proj), ("blk", "col")
+            lax.psum((jnp.sum(residual_now * residual_now, axis=0), local_proj), "blk"), "col"
         )
         coefficients = jax.scipy.linalg.cho_solve((gram_chol, True), projection)
         scaled = (

time: 1040 us -> 1080 us (1.038)
  waiting for transfers between devices: 309 us -> 359 us
    psum x1, waiting for transfers between devices: 93 us -> 136 us  [per_device(): gram = lax.psum(local_gram, ('blk', 'col'))]
    psum x2 -> x6, waiting for transfers between devices: 158 us -> 184 us  [the longest x3 169 us: precondition(): lax.psum((jnp.sum(residual_now * residual_now, axis=0), local_proj), 'blk')]
    reduce_scatter x3, waiting for transfers between devices: 57.5 us -> 39.1 us  [per_device(): lax.psum_scatter(result, 'col', scatter_dimension=0, tiled=True)]
    psum x2 -> x6, blocking collectives: 82.2 us -> 78.5 us  [the longest x3 61.1 us: precondition(): lax.psum((jnp.sum(residual_now * residual_now, axis=0), local_proj), 'blk')]
  transfers between devices with their start and end apart: 6 -> 10, of which waited for: 6 -> 8; matrix products, arithmetic and copies ran while one was open for 0% -> 13% of each run, Pallas kernels for 0% -> 0%
where the time goes in v1:
time: 1080 us; the launch traced here: 1070 us
  blocking collectives  367 us (34%)
  waiting for transfers between devices  359 us (33%)
  other arithmetic  234 us (22%)
  matrix products  59.1 us (5%)
  local copies, waits for them, and re-layouts  27.6 us (3%)
  between operations  21.1 us (2%)
    psum x3, waiting for transfers between devices, precondition(): lax.psum((jnp.sum(residual_now * residual_now, axis=0), local_proj), 'blk')  169 us
    psum x1, waiting for transfers between devices, per_device(): gram = lax.psum(local_gram, ('blk', 'col'))  136 us
    psum x3, blocking collectives, per_device(): curvature = lax.psum(jnp.sum(direction_now * image, axis=0), ('blk', 'col'))  115 us
    all_gather x3, blocking collectives, per_device(): lax.all_gather(direction_now, 'blk', axis=0, tiled=True)  91.8 us
    another operation x15, other arithmetic, per_device(): gram_chol = jnp.linalg.cholesky(gram)  79.2 us
    psum x3, blocking collectives, precondition(): lax.psum((jnp.sum(residual_now * residual_now, axis=0), local_proj), 'blk')  61.1 us
    psum x1, blocking collectives, per_device(): picked = lax.psum(local_pick, ('blk', 'col')).astype(jnp.bfloat16)  44.6 us
    another operation x4, other arithmetic, precondition(): coefficients = jax.scipy.linalg.cho_solve((gram_chol, True), projection)  40.3 us
  transfers between devices with their start and end apart: 10, of which 8 were waited for; matrix products, arithmetic and copies ran while one was open for 13% of the time, Pallas kernels for 0%

profile of v1, /device:TPU:0, one launch (start us, length us, event | category | flops | bytes accessed | tf_op | source)
XLA Modules:
  0.0 1069.5 jit_solution(4703764759442106833)
XLA Ops:
  8.9 44.6 %all-reduce.24 = bf16[512,128]{1,0:T(8,128)(2,1)S(1)} all-reduce(f32[512,128]{1,0:T(8,128)S(1)} %fusion.59), channel_id=1, replica_groups=mesh['blk'=8,'col'=4] {'blk','col'}, use_global_device_ids=true, to_apply=%region_0.0 | all-reduce | flops 65536 | bytes 393216 | tf_op jit(solution)/shard_map/psum | solution.py:67
  54.1 11.7 %cholesky.354 = f32[128,128]{1,0:T(8,128)S(1)} custom-call(f32[128,128]{1,0:T(8,128)S(1)} %cholesky.404), custom_call_target="Cholesky" | custom-call | tf_op jit(solution)/shard_map/jit(cholesky)/cholesky | solution.py:35
  76.4 11.7 %cholesky.364 = f32[128,128]{1,0:T(8,128)S(1)} custom-call(f32[128,128]{1,0:T(8,128)S(1)} %convolution_subtract_fusion.8), custom_call_target="Cholesky" | custom-call | tf_op jit(solution)/shard_map/jit(cholesky)/cholesky | solution.py:35
  96.3 19.7 %custom-call.55 = f32[2,128,128]{1,2,0:T(8,128)S(1)} custom-call(f32[2,128,128]{2,1,0:T(8,128)S(1)} %get-tuple-element.391), custom_call_target="InvertDiagBlocksLowerTriangular" | custom-call | tf_op jit(solution)/shard_map/jit(_solve_triangular)/triangular_solve | solution.py:27
  118.7 11.7 %cholesky.381 = f32[128,128]{1,0:T(8,128)S(1)} custom-call(f32[128,128]{1,0:T(8,128)S(1)} %cholesky.407), custom_call_target="Cholesky" | custom-call | tf_op jit(solution)/shard_map/jit(cholesky)/cholesky | solution.py:49
  140.8 11.7 %cholesky.391 = f32[128,128]{1,0:T(8,128)S(1)} custom-call(f32[128,128]{1,0:T(8,128)S(1)} %convolution_subtract_fusion.6), custom_call_target="Cholesky" | custom-call | tf_op jit(solution)/shard_map/jit(cholesky)/cholesky | solution.py:49
  159.6 19.7 %custom-call.57 = f32[2,128,128]{1,2,0:T(8,128)S(1)} custom-call(f32[2,128,128]{2,1,0:T(8,128)S(1)} %get-tuple-element.392), custom_call_target="InvertDiagBlocksLowerTriangular" | custom-call | tf_op jit(solution)/shard_map/jit(_solve_triangular)/triangular_solve | solution.py:27
  190.0 30.7 %all_gather.18 = bf16[1024,128]{1,0:T(8,128)(2,1)S(1)} all-gather(bf16[128,128]{1,0:T(8,128)(2,1)S(1)} %copy-done.6), channel_id=1, replica_groups=mesh['blk'=8,'col'=4] {'blk'}, dimensions={0}, use_global_device_ids=true | all-gather | bytes 294912 | tf_op jit(solution)/shard_map/all_gather | solution.py:102
  221.6 29.2 %all-reduce.13.cloned.1.call-done = f32[512,32]{0,1:T(8,128)} async-done(((f32[512,32]{0,1:T(8,128)}), f32[512,32]{0,1:T(8,128)}) %all-reduce.13.cloned.1.call-update) | async-done | bytes 65552 | tf_op jit(solution)/shard_map/psum | solution.py:82
  251.0 135.9 %all-reduce.11.cloned.1.call-done = f32[512,512]{1,0:T(8,128)} async-done(((f32[512,512]{1,0:T(8,128)}), f32[512,512]{1,0:T(8,128)}) %all-reduce.11.cloned.1.call-update) | async-done | bytes 1048592 | tf_op jit(solution)/shard_map/psum | solution.py:73
  389.7 11.7 %cholesky.166 = f32[128,128]{1,0:T(8,128)S(1)} custom-call(f32[128,128]{1,0:T(8,128)S(1)} %cholesky.410), custom_call_target="Cholesky" | custom-call | tf_op jit(solution)/shard_map/jit(cholesky)/cholesky | solution.py:75
  412.1 11.7 %cholesky.189 = f32[128,128]{1,0:T(8,128)S(1)} custom-call(f32[128,128]{1,0:T(8,128)S(1)} %cholesky.414), custom_call_target="Cholesky" | custom-call | tf_op jit(solution)/shard_map/jit(cholesky)/cholesky | solution.py:75
  435.7 11.7 %cholesky.292 = f32[128,128]{1,0:T(8,128)S(1)} custom-call(f32[128,128]{1,0:T(8,128)S(1)} %cholesky.419), custom_call_target="Cholesky" | custom-call | tf_op jit(solution)/shard_map/jit(cholesky)/cholesky | solution.py:75
  458.6 11.7 %cholesky.305 = f32[128,128]{1,0:T(8,128)S(1)} custom-call(f32[128,128]{1,0:T(8,128)S(1)} %convolution_subtract_fusion.9), custom_call_target="Cholesky" | custom-call | tf_op jit(solution)/shard_map/jit(cholesky)/cholesky | solution.py:75
  473.9 10.4 while.55
  484.3 40.1 %custom-call.59 = f32[4,128,128]{1,2,0:T(8,128)S(1)} custom-call(f32[4,128,128]{2,1,0:T(8,128)} %get-tuple-element.393), custom_call_target="InvertDiagBlocksLowerTriangular" | custom-call | tf_op jit(solution)/shard_map/jit(_cho_solve)/triangular_solve | solution.py:84
  529.2 30.5 %all_gather.19 = f32[1024,32]{0,1:T(8,128)S(1)} all-gather(f32[128,32]{0,1:T(8,128)S(1)} %get-tuple-element.534), channel_id=1, replica_groups=mesh['blk'=8,'col'=4] {'blk'}, dimensions={0}, use_global_device_ids=true | all-gather | bytes 147456 | tf_op jit(solution)/shard_map/all_gather | solution.py:105
  560.6 11.4 %while.50 = (s32[]{:T(128)}, f32[512,32]{0,1:T(8,128)S(1)}, f32[512]{0:T(512)S(1)}, f32[8,128]{1,0:T(8,128)S(1)}, bf16[8,128,128]{2,1,0:T(8,128)(2,1)}, /*index=...) while((s32[]{:T(128)}, f32[512,32]{0,1:T(8,128)S(1)}, ...), condition=%wide.region_26.31_spmd.clone, body=%wide.region_25.30_spmd.clone.sunk | while | flops 42237952 | bytes 888943 | solution.py:117
  572.7 20.4 %psum.123 = f32[32]{0:T(128)S(1)} all-reduce(f32[32]{0:T(128)S(1)} %multiply_reduce_fusion.13), channel_id=1, replica_groups=mesh['blk'=8,'col'=4] {'blk'}, use_global_device_ids=true, to_apply=%region_20.25 | all-reduce | flops 32 | bytes 256 | tf_op jit(solution)/shard_map/psum | solution.py:82
  599.9 36.9 %psum.125 = f32[32]{0:T(128)S(1)} all-reduce(f32[32]{0:T(128)S(1)} %get-tuple-element.502), channel_id=1, replica_groups=mesh['blk'=8,'col'=4] {'blk','col'}, use_global_device_ids=true, to_apply=%region_29.34 | all-reduce | flops 32 | bytes 256 | tf_op jit(solution)/shard_map/psum | solution.py:122
  638.1 69.8 %all-reduce.17.cloned.1.call-done = f32[512,32]{0,1:T(8,128)} async-done(((f32[512,32]{0,1:T(8,128)}), f32[512,32]{0,1:T(8,128)}) %all-reduce.17.cloned.1.call-update) | async-done | bytes 65552 | tf_op jit(solution)/shard_map/psum | solution.py:82
  707.9 20.4 %psum.126 = f32[32]{0:T(128)S(1)} all-reduce(f32[32]{0:T(128)S(1)} %get-tuple-element.500), channel_id=1, replica_groups=mesh['blk'=8,'col'=4] {'blk'}, use_global_device_ids=true, to_apply=%region_31.36 | all-reduce | flops 32 | bytes 256 | tf_op jit(solution)/shard_map/psum | solution.py:82
  745.9 30.7 %all_gather.20 = f32[1024,32]{0,1:T(8,128)S(1)} all-gather(f32[128,32]{0,1:T(8,128)S(1)} %fusion.53), channel_id=1, replica_groups=mesh['blk'=8,'col'=4] {'blk'}, dimensions={0}, use_global_device_ids=true | all-gather | bytes 147456 | tf_op jit(solution)/shard_map/all_gather | solution.py:105
  776.8 11.4 %while.51 = (s32[]{:T(128)}, f32[512,32]{0,1:T(8,128)S(1)}, f32[512]{0:T(512)S(1)}, f32[8,128]{1,0:T(8,128)S(1)}, bf16[8,128,128]{2,1,0:T(8,128)(2,1)}, /*index=...) while((s32[]{:T(128)}, f32[512,32]{0,1:T(8,128)S(1)}, ...), condition=%wide.region_37.42_spmd.clone, body=%wide.region_36.41_spmd.clone.sunk | while | flops 42237952 | bytes 888943 | solution.py:117
  788.9 19.5 %reduce-scatter.6.cloned.1.call-done = f32[128,32]{0,1:T(8,128)} async-done(((f32[512,32]{0,1:T(8,128)}), f32[128,32]{0,1:T(8,128)}) %reduce-scatter.6.cloned.1.call-update) | async-done | bytes 16400 | tf_op jit(solution)/shard_map/reduce_scatter | solution.py:119
  809.3 39.3 %psum.130 = f32[32]{0:T(128)S(1)} all-reduce(f32[32]{0:T(128)S(1)} %multiply_reduce_fusion.10), channel_id=1, replica_groups=mesh['blk'=8,'col'=4] {'blk','col'}, use_global_device_ids=true, to_apply=%region_40.45 | all-reduce | flops 32 | bytes 256 | tf_op jit(solution)/shard_map/psum | solution.py:122
  849.9 70.1 %all-reduce.21.cloned.1.call-done = f32[512,32]{0,1:T(8,128)} async-done(((f32[512,32]{0,1:T(8,128)}), f32[512,32]{0,1:T(8,128)}) %all-reduce.21.cloned.1.call-update) | async-done | bytes 65552 | tf_op jit(solution)/shard_map/psum | solution.py:82
  920.0 20.4 %psum.131 = f32[32]{0:T(128)S(1)} all-reduce(f32[32]{0:T(128)S(1)} %get-tuple-element.498), channel_id=1, replica_groups=mesh['blk'=8,'col'=4] {'blk'}, use_global_device_ids=true, to_apply=%region_42.47 | all-reduce | flops 32 | bytes 256 | tf_op jit(solution)/shard_map/psum | solution.py:82
  958.2 30.7 %all_gather.21 = f32[1024,32]{0,1:T(8,128)S(1)} all-gather(f32[128,32]{0,1:T(8,128)S(1)} %fusion.54), channel_id=1, replica_groups=mesh['blk'=8,'col'=4] {'blk'}, dimensions={0}, use_global_device_ids=true | all-gather | bytes 147456 | tf_op jit(solution)/shard_map/all_gather | solution.py:105
  989.1 11.4 %while.52 = (s32[]{:T(128)}, f32[512,32]{0,1:T(8,128)S(1)}, f32[512]{0:T(512)S(1)}, f32[8,128]{1,0:T(8,128)S(1)}, bf16[8,128,128]{2,1,0:T(8,128)(2,1)}, /*index=...) while((s32[]{:T(128)}, f32[512,32]{0,1:T(8,128)S(1)}, ...), condition=%wide.region_48.53_spmd.clone, body=%wide.region_47.52_spmd.clone.sunk | while | flops 42237952 | bytes 888943 | solution.py:117
  1001.1 19.6 %reduce-scatter.8.cloned.1.call-done = f32[128,32]{0,1:T(8,128)} async-done(((f32[512,32]{0,1:T(8,128)}), f32[128,32]{0,1:T(8,128)}) %reduce-scatter.8.cloned.1.call-update) | async-done | bytes 16400 | tf_op jit(solution)/shard_map/reduce_scatter | solution.py:119
  1022.3 39.2 %psum.135 = f32[32]{0:T(128)S(1)} all-reduce(f32[32]{0:T(128)S(1)} %multiply_reduce_fusion.8), channel_id=1, replica_groups=mesh['blk'=8,'col'=4] {'blk','col'}, use_global_device_ids=true, to_apply=%region_51.56 | all-reduce | flops 32 | bytes 256 | tf_op jit(solution)/shard_map/psum | solution.py:122
  (315 shorter events, 194.6 us)
Async XLA Ops:
  7.2 243.7 %all-reduce.13.cloned.1.call-start = ((), (), s32[]{:S(2)}) async-start(), calls=%async_computation.4 | async-start | bytes 131072 | tf_op jit(solution)/shard_map/psum | solution.py:82
  7.2 0.7 copy-start.14
  88.1 0.8 copy-start.6
  180.6 0.7 copy-start.10
  182.4 204.5 %all-reduce.11.cloned.1.call-start = ((), (), s32[]{:S(2)}) async-start(), calls=%async_computation.3 | async-start | bytes 2097152 | tf_op jit(solution)/shard_map/psum | solution.py:73
  184.5 339.9 %all-reduce.15.cloned.1.call-start = ((), (), s32[]{:S(2)}) async-start(), calls=%async_computation.5 | async-start | bytes 131072 | tf_op jit(solution)/shard_map/psum | solution.py:81
  220.7 0.7 copy-start.1
  250.9 348.2 %reduce-scatter.4.cloned.1.call-start = ((), (), s32[]{:S(2)}) async-start(), calls=%async_computation.6 | async-start | bytes 81920 | tf_op jit(solution)/shard_map/reduce_scatter | solution.py:119
  388.2 1.2 copy-start
  524.4 1.0 copy-start.7
  528.2 0.7 copy-start.11
  559.7 0.8 copy-start.2
  571.9 0.6 copy-start.3
  572.6 135.2 %all-reduce.17.cloned.1.call-start = ((), (), s32[]{:S(2)}) async-start(), calls=%async_computation.7 | async-start | bytes 131072 | tf_op jit(solution)/shard_map/psum | solution.py:82
  638.0 103.5 %all-reduce.19.cloned.1.call-start = ((), (), s32[]{:S(2)}) async-start(), calls=%async_computation.8 | async-start | bytes 131072 | tf_op jit(solution)/shard_map/psum | solution.py:81
  707.8 100.5 %reduce-scatter.6.cloned.1.call-start = ((), (), s32[]{:S(2)}) async-start(), calls=%async_computation.9 | async-start | bytes 81920 | tf_op jit(solution)/shard_map/reduce_scatter | solution.py:119
  741.5 1.0 copy-start.9
  788.2 0.6 copy-start.5
  788.8 131.2 %all-reduce.21.cloned.1.call-start = ((), (), s32[]{:S(2)}) async-start(), calls=%async_computation.10 | async-start | bytes 131072 | tf_op jit(solution)/shard_map/psum | solution.py:82
  808.4 40.2 %copy-start.13 = (f32[128,32]{0,1:T(8,128)S(1)}, f32[128,32]{0,1:T(8,128)}, u32[]{:S(2)}) copy-start(f32[128,32]{0,1:T(8,128)} %reduce-scatter.6.cloned.1.call-done) | copy-start | bytes 49156
  849.8 104.0 %all-reduce.23.cloned.1.call-start = ((), (), s32[]{:S(2)}) async-start(), calls=%async_computation.11 | async-start | bytes 131072 | tf_op jit(solution)/shard_map/psum | solution.py:81
  920.0 100.7 %reduce-scatter.8.cloned.1.call-start = ((), (), s32[]{:S(2)}) async-start(), calls=%async_computation.12 | async-start | bytes 81920 | tf_op jit(solution)/shard_map/reduce_scatter | solution.py:119
  953.8 1.0 copy-start.8
  1000.5 0.6 copy-start.4
  1021.5 40.0 %copy-start.12 = (f32[128,32]{0,1:T(8,128)S(1)}, f32[128,32]{0,1:T(8,128)}, u32[]{:S(2)}) copy-start(f32[128,32]{0,1:T(8,128)} %reduce-scatter.8.cloned.1.call-done) | copy-start | bytes 49156
Sparse Core Ops, SparseCore 0:
  182.5 68.3 all-reduce.12
  256.1 130.7 all-reduce.10
  389.2 30.7 all-reduce.14
  572.7 18.5 reduce-scatter.3
  638.1 69.6 all-reduce.16
  710.0 31.4 all-reduce.18
  788.9 19.3 reduce-scatter.5
  849.9 69.9 all-reduce.20
  922.3 31.4 all-reduce.22
  1001.2 19.4 reduce-scatter.7
